TPU v7x, 1024 devices: a whole 4x4x32 slice. The times are simulated.
1024 devices in a mesh: row: 16 (over x_hi, y, core), col: 64 (over z, x_lo).
Axes of the slice: x: 4 (x_hi: 2, x_lo: 2; x = x_hi * 2 + x_lo), y: 4, z: 32, core: 2. Of those that a mesh axis runs over, the one named last changes fastest.
Arguments:
- start_block: bfloat16 [131072, 128], P(('row', 'col')), may hold values from -6 to 6
- matrix_tiles: bfloat16 [16, 16, 64, 2, 128, 128], P('row', None, 'col')
- tile_columns: int32 [16, 16, 64, 2], P('row', None, 'col'), may hold values from 0 to 63
- history: bfloat16 [131072, 512], P(('row', 'col'))
Outputs:
- new_block: float32 [131072, 128], P(('row', 'col'))
- coeffs: float32 [512, 128], replicated
All inputs are finite; a program needn't handle non-finite values.
Results may differ from a plain program's by a relative error of at most 0.0029.
Values may be sent and summed in bfloat16 or wider, within the bound.
A program may use at most 32 MiB of HBM per device.

v0:
```python
import functools

import jax
import jax.numpy as jnp
from jax import lax
from jax.sharding import Mesh
from jax.sharding import PartitionSpec as P

COL = ("col_0", "col_1")
ROW = ("row_0", "row_1", "row_2")
ROW_COL = ("row_0", "row_1", "row_2", "col_0", "col_1")


def gathered_by_axis(value, axes, dim):
    if not axes:
        return value
    nearer = lax.all_gather(value, axes[-1], axis=dim, tiled=True)
    return gathered_by_axis(nearer, axes[:-1], dim)


def split_up(value, dim, peers):
    before, after = (value.shape[:dim], value.shape[dim + 1 :])
    return jnp.moveaxis(value.reshape(*before, peers, -1, *after), dim, 0)


def sum_at_owner(value, axis, dim):
    blocks = split_up(value, dim, lax.axis_size(axis))
    arrived = lax.all_to_all(blocks, axis, split_axis=0, concat_axis=0, tiled=True)
    return arrived.sum(axis=0)


def one_axis_at_a_time(value, axes):
    return functools.reduce(lax.psum, axes, value)


def apply_matrix(pieces, matrix_tiles, tile_columns):
    gathered = gathered_by_axis(pieces, COL, 0)
    tile_order = matrix_tiles.shape[-1]
    block_width = gathered.shape[1]
    column_count = gathered.shape[0] // tile_order
    blocks = gathered.reshape(column_count, tile_order, block_width)
    picked = blocks[tile_columns[0, :, 0, :]]
    local_tiles = matrix_tiles[0, :, 0]
    partial_value = jnp.einsum(
        "rsij,rsjk->rik", local_tiles, picked, preferred_element_type=jnp.float32
    )
    partial_value = partial_value.reshape(partial_value.shape[0] * tile_order, block_width)
    return sum_at_owner(partial_value, ROW, 0)


def per_device(start_block, matrix_tiles, tile_columns, history):
    history_wide = history.astype(jnp.float32)
    start_wide = start_block.astype(jnp.float32)
    first_power = apply_matrix(start_block, matrix_tiles, tile_columns).astype(jnp.bfloat16)
    second_power = apply_matrix(first_power, matrix_tiles, tile_columns)
    filtered = 2.0 * second_power - start_wide
    coeffs = one_axis_at_a_time(
        jnp.dot(history_wide.T, filtered, precision=lax.Precision.HIGHEST), ROW_COL
    )
    cleaned = filtered - jnp.dot(history_wide, coeffs, precision=lax.Precision.HIGHEST)
    squares = one_axis_at_a_time(jnp.sum(cleaned * cleaned, axis=0), ROW_COL)
    row_total = cleaned.shape[0] * lax.axis_size(ROW) * lax.axis_size(COL)
    lengths = jnp.sqrt(squares / row_total + 1e-05)
    return (cleaned / lengths[None, :], coeffs)


def solution(mesh):
    split = Mesh(
        mesh.devices.reshape(2, 4, 2, 32, 2), ("row_0", "row_1", "row_2", "col_0", "col_1")
    )
    return jax.shard_map(
        per_device,
        mesh=split,
        in_specs=(
            P(ROW_COL, None),
            P(ROW, None, COL, None, None, None),
            P(ROW, None, COL, None),
            P(ROW_COL, None),
        ),
        out_specs=(P(ROW_COL, None), P()),
        check_vma=False,
    )
```

profile of v0, /device:TPU:1, one launch (start us, length us, event | category | flops | bytes accessed | tf_op | source)
XLA Modules:
  0.0 961.2 jit_solution(17210549394980761789)
XLA Ops:
  7.2 5.8 all_gather.12
  13.1 0.7 compare_select_fusion
  14.0 125.1 %all-gather.3.cloned.1.call-done = bf16[8192,128]{1,0:T(8,128)(2,1)} async-done(((bf16[256,128]{1,0:T(8,128)(2,1)}), bf16[8192,128]{1,0:T(8,128)(2,1)}) %all-gather.3.cloned.1.call-update) | async-done | bytes 2097168 | tf_op jit(solution)/shard_map/all_gather | solution.py:17
  139.0 2.3 gather_fusion
  141.9 44.6 %all_to_all.10 = f32[16,128,128]{1,2,0:T(8,128)S(1)} all-to-all(f32[16,128,128]{1,2,0:T(8,128)S(1)} %convolution_bitcast_fusion.1), channel_id=1, replica_groups=mesh['row_0'=2,'row_1'=4,'row_2'=2,'col_0'=32,'col_1'=2] {'row_0','row_1..., dimensions={0} | all-to-all | bytes 2097152 | tf_op jit(solution)/shard_map/all_to_all | solution.py:28
  186.5 3.6 all_gather.14
  190.1 107.1 %all-gather.5.cloned.1.call-done = bf16[8192,128]{0,1:T(8,128)(2,1)} async-done(((bf16[256,128]{0,1:T(8,128)(2,1)}), bf16[8192,128]{0,1:T(8,128)(2,1)}) %all-gather.5.cloned.1.call-update) | async-done | bytes 2097168 | tf_op jit(solution)/shard_map/all_gather | solution.py:17
  297.2 3.2 copy.15
  300.4 1.7 gather_fusion.1
  302.1 1.7 convolution_bitcast_fusion
  303.8 47.8 %all_to_all.11 = f32[16,128,128]{1,2,0:T(8,128)S(1)} all-to-all(f32[16,128,128]{1,2,0:T(8,128)S(1)} %convolution_bitcast_fusion), channel_id=1, replica_groups=mesh['row_0'=2,'row_1'=4,'row_2'=2,'col_0'=32,'col_1'=2] {'row_0','row_1..., dimensions={0} | all-to-all | bytes 2097152 | tf_op jit(solution)/shard_map/all_to_all | solution.py:28
  351.8 1.0 convolution_bitcast_fusion.2
  352.9 53.9 %all-reduce.6.cloned.1.call-done = f32[512,128]{0,1:T(8,128)} async-done(((f32[512,128]{0,1:T(8,128)}), f32[512,128]{0,1:T(8,128)}) %all-reduce.6.cloned.1.call-update) | async-done | bytes 262160 | tf_op jit(solution)/shard_map/psum | solution.py:33
  406.8 78.3 %all-reduce.8.cloned.1.call-done = f32[512,128]{0,1:T(8,128)} async-done(((f32[512,128]{0,1:T(8,128)}), f32[512,128]{0,1:T(8,128)}) %all-reduce.8.cloned.1.call-update) | async-done | bytes 262160 | tf_op jit(solution)/shard_map/psum | solution.py:33
  485.2 68.6 %all-reduce.10.cloned.1.call-done = f32[512,128]{0,1:T(8,128)} async-done(((f32[512,128]{0,1:T(8,128)}), f32[512,128]{0,1:T(8,128)}) %all-reduce.10.cloned.1.call-update) | async-done | bytes 262160 | tf_op jit(solution)/shard_map/psum | solution.py:33
  553.8 246.4 %all-reduce.12.cloned.1.call-done = f32[512,128]{0,1:T(8,128)} async-done(((f32[512,128]{0,1:T(8,128)}), f32[512,128]{0,1:T(8,128)}) %all-reduce.12.cloned.1.call-update) | async-done | bytes 262160 | tf_op jit(solution)/shard_map/psum | solution.py:33
  800.3 80.4 %all-reduce.14.cloned.1.call-done = f32[512,128]{0,1:T(8,128)} async-done(((f32[512,128]{0,1:T(8,128)}), f32[512,128]{0,1:T(8,128)}) %all-reduce.14.cloned.1.call-update) | async-done | bytes 262160 | tf_op jit(solution)/shard_map/psum | solution.py:33
  880.7 1.2 multiply_reduce_fusion
  881.9 5.3 psum.75
  887.2 8.7 psum.76
  895.8 6.2 psum.77
  902.1 46.1 %psum.78 = f32[128]{0:T(128)S(1)} all-reduce(f32[128]{0:T(128)S(1)} %psum.77), channel_id=1, replica_groups=mesh['row_0'=2,'row_1'=4,'row_2'=2,'col_0'=32,'col_1'=2] {'col_0'}, use_global_device_ids=true, to_apply=%region_11.0 | all-reduce | flops 128 | bytes 1024 | tf_op jit(solution)/shard_map/psum | solution.py:33
  948.1 3.8 psum.79
  952.6 1.8 copy.18
  (29 shorter events, 1.9 us)
Async XLA Ops:
  7.2 134.2 %copy-start = (bf16[1,16,1,2,128,128]{5,4,3,2,1,0:T(8,128)(2,1)S(1)}, bf16[1,16,1,2,128,128]{5,4,3,2,1,0:T(8,128)(2,1)}, u32[]{:S(2)}) copy-start(bf16[1,16,1,2,128,128]{5,4,3,2,1,0:T(8,128)(2,1)} %param.5) | copy-start | bytes 3145732
  7.2 131.8 %all-gather.3.cloned.1.call-start = ((), (), s32[]{:S(2)}) async-start(), calls=%async_computation.2 | async-start | bytes 2162688 | tf_op jit(solution)/shard_map/all_gather | solution.py:17
  13.0 284.1 %all-gather.5.cloned.1.call-start = ((), (), s32[]{:S(2)}) async-start(), calls=%async_computation.3 | async-start | bytes 2162688 | tf_op jit(solution)/shard_map/all_gather | solution.py:17
  190.1 216.7 %all-reduce.6.cloned.1.call-start = ((), (), s32[]{:S(2)}) async-start(), calls=%async_computation.4 | async-start | bytes 524288 | tf_op jit(solution)/shard_map/psum | solution.py:33
  303.8 47.9 %copy-start.1 = (bf16[128,512]{1,0:T(8,128)(2,1)S(1)}, bf16[128,512]{1,0:T(8,128)(2,1)}, u32[]{:S(2)}) copy-start(bf16[128,512]{1,0:T(8,128)(2,1)} %param.7) | copy-start | bytes 393220
  303.8 47.9 %copy-start.2 = (bf16[128,128]{1,0:T(8,128)(2,1)S(1)}, bf16[128,128]{1,0:T(8,128)(2,1)}, u32[]{:S(2)}) copy-start(bf16[128,128]{1,0:T(8,128)(2,1)} %param.4) | copy-start | bytes 98308
  352.8 132.3 %all-reduce.8.cloned.1.call-start = ((), (), s32[]{:S(2)}) async-start(), calls=%async_computation.5 | async-start | bytes 524288 | tf_op jit(solution)/shard_map/psum | solution.py:33
  406.8 147.0 %all-reduce.10.cloned.1.call-start = ((), (), s32[]{:S(2)}) async-start(), calls=%async_computation.6 | async-start | bytes 524288 | tf_op jit(solution)/shard_map/psum | solution.py:33
  485.1 315.1 %all-reduce.12.cloned.1.call-start = ((), (), s32[]{:S(2)}) async-start(), calls=%async_computation.7 | async-start | bytes 524288 | tf_op jit(solution)/shard_map/psum | solution.py:33
  553.8 326.9 %all-reduce.14.cloned.1.call-start = ((), (), s32[]{:S(2)}) async-start(), calls=%async_computation.8 | async-start | bytes 524288 | tf_op jit(solution)/shard_map/psum | solution.py:33
Sparse Core Ops, SparseCore 0:
  13.2 125.8 all-gather.2
  190.2 106.9 all-gather.4
  352.9 53.7 all-reduce.5
  408.9 76.1 all-reduce.7
  488.4 65.3 all-reduce.9
  555.9 244.2 all-reduce.11
  803.7 76.9 all-reduce.13
where the time goes:
time: 974 us; the launch traced here: 961 us
  waiting for transfers between devices  760 us (78%)
  blocking collectives  172 us (18%)
  between operations  14.2 us (1%)
    psum x5, waiting for transfers between devices, one_axis_at_a_time(): return functools.reduce(lax.psum, axes, value)  528 us
    all_gather x2, waiting for transfers between devices, gathered_by_axis(): nearer = lax.all_gather(value, axes[-1], axis=dim, tiled=True)  232 us
    all_to_all x2, blocking collectives, sum_at_owner(): lax.all_to_all(blocks, axis, split_axis=0, concat_axis=0, tiled=True)  92.3 us
    psum x5, blocking collectives, one_axis_at_a_time(): return functools.reduce(lax.psum, axes, value)  70 us
  transfers between devices with their start and end apart: 7, of which 7 were waited for; matrix products, arithmetic and copies ran while one was open for 0% of the time, Pallas kernels for 0%

commit v1 on v0

v1 whole, which is shorter than its diff:
```python
import functools

import jax
import jax.numpy as jnp
from jax import lax
from jax.experimental import pallas as pl
from jax.experimental.pallas import tpu as pltpu
from jax.sharding import Mesh
from jax.sharding import PartitionSpec as P

COL = ("col_0", "col_1")
ROW = ("row_0", "row_1", "row_2")
ROW_COL = ROW + COL
MESH = pl.DeviceIdType.MESH
XH, Y, CORE, Z, XL = 2, 4, 2, 32, 2
ZA = 8
ZB = Z // ZA
PLANE = XH * XL * Y * CORE
TILE = 128


def split3(x):
    hi = x.astype(jnp.bfloat16)
    rest = x - hi.astype(jnp.float32)
    mid = rest.astype(jnp.bfloat16)
    low = (rest - mid.astype(jnp.float32)).astype(jnp.bfloat16)
    return hi, mid, low


def wait_bytes(ref, sem):
    pltpu.make_async_copy(ref, ref, sem).wait()


def kernel(
    states,
    cols,
    start,
    tiles,
    hist,
    out,
    coef_out,
    seg1,
    seg2,
    part,
    core_in,
    summed,
    y_in,
    pair,
    x_in,
    filt,
    proj,
    proj_in,
    za_in,
    zb_in,
    coef,
    sq_plane,
    sq_z,
    ring_send,
    ring_recv,
    row_send,
    row_recv,
    group_send,
    group_recv,
    local_sem,
):
    xh, y, core = (lax.axis_index(a) for a in ROW)
    z, xl = (lax.axis_index(a) for a in COL)
    right = (xh, y, core, lax.rem(z + 1, Z), xl)
    left = (xh, y, core, lax.rem(z + Z - 1, Z), xl)
    across = (xh, y, core, z, 1 - xl)
    place = ((xh * XL + xl) * Y + y) * CORE + core

    def plane_device(q):
        return (
            q // (XL * Y * CORE),
            lax.rem(q // CORE, Y),
            lax.rem(q, CORE),
            z,
            lax.rem(q // (Y * CORE), XL),
        )

    barrier = pltpu.get_barrier_semaphore()

    def greet(i, carry):
        device = plane_device(lax.rem(place + i, PLANE))
        pl.semaphore_signal(barrier, inc=1, device_id=device, device_id_type=MESH)
        return carry

    for device in (left, right):
        pl.semaphore_signal(barrier, inc=1, device_id=device, device_id_type=MESH)
    lax.fori_loop(1, PLANE, greet, 0)
    pl.semaphore_wait(barrier, PLANE + 1)

    def slot_of(zz):
        return lax.rem(zz + Z, Z) * XL + xl

    def gather(seg, which):
        def send(slot, device, lane):
            pltpu.make_async_remote_copy(
                src_ref=seg.at[slot],
                dst_ref=seg.at[slot],
                send_sem=ring_send.at[which, lane],
                recv_sem=ring_recv.at[which, slot],
                device_id=device,
                device_id_type=MESH,
            ).start()

        def arrived(slot):
            wait_bytes(seg.at[slot], ring_recv.at[which, slot])

        def step(k, carry):
            ahead, behind = slot_of(z - k), slot_of(z + k)
            send(ahead, right, 0)
            send(behind, left, 1)
            send(ahead, across, 2)

            @pl.when(k > 0)
            def _():
                send(behind, across, 2)

            arrived(slot_of(z - k - 1))
            arrived(slot_of(z + k + 1))
            return carry

        half = Z // 2
        lax.fori_loop(0, half - 1, step, 0)
        send(slot_of(z - half + 1), right, 0)
        send(slot_of(z - half + 1), across, 2)
        send(slot_of(z + half - 1), across, 2)
        arrived(slot_of(z - half))
        send(slot_of(z - half), across, 2)

        def other(zz, carry):
            arrived(zz * XL + 1 - xl)
            return carry

        lax.fori_loop(0, Z, other, 0)
        wait_bytes(seg.at[pl.ds(0, half)], ring_send.at[which, 0])
        wait_bytes(seg.at[pl.ds(0, half - 1)], ring_send.at[which, 1])
        wait_bytes(seg.at[pl.ds(0, Z)], ring_send.at[which, 2])

    def multiply(seg, which):
        def one(owner_core, yy, xx):
            p = (xx * Y + yy) * CORE + owner_core
            total = jnp.dot(
                tiles[p, 0], seg[cols[p, 0]], preferred_element_type=jnp.float32
            )
            total += jnp.dot(
                tiles[p, 1], seg[cols[p, 1]], preferred_element_type=jnp.float32
            )
            part[owner_core, yy, xx] = total

        def half_of(owner_core):
            def body(yy, carry):
                for xx in range(XH):
                    one(owner_core, yy, xx)
                return carry

            lax.fori_loop(0, Y, body, 0)

        half_of(1 - core)
        swap = pltpu.make_async_remote_copy(
            src_ref=part.at[1 - core],
            dst_ref=core_in.at[which],
            send_sem=row_send.at[which, 0],
            recv_sem=row_recv.at[which, 0],
            device_id=(xh, y, 1 - core, z, xl),
            device_id_type=MESH,
        )
        swap.start()
        half_of(core)
        swap.wait()

        def add_up(yy, carry):
            summed[yy] = part[core, yy] + core_in[which, yy]
            return carry

        lax.fori_loop(0, Y, add_up, 0)
        hops = []
        for i in (2, 1, 3):
            hops.append(
                pltpu.make_async_remote_copy(
                    src_ref=summed.at[lax.rem(y + i, Y)],
                    dst_ref=y_in.at[which, i - 1],
                    send_sem=row_send.at[which, i],
                    recv_sem=row_recv.at[which, i],
                    device_id=(xh, lax.rem(y + i, Y), core, z, xl),
                    device_id_type=MESH,
                )
            )
        for hop in hops:
            hop.start()
        for hop in hops:
            hop.wait()
        pair[...] = summed[y] + y_in[which, 0] + y_in[which, 1] + y_in[which, 2]
        last = pltpu.make_async_remote_copy(
            src_ref=pair.at[1 - xh],
            dst_ref=x_in.at[which],
            send_sem=row_send.at[which, Y],
            recv_sem=row_recv.at[which, Y],
            device_id=(1 - xh, y, core, z, xl),
            device_id_type=MESH,
        )
        last.start()
        last.wait()
        return pair[xh] + x_in[which]

    mine = slot_of(z)
    first = pltpu.make_async_copy(start, seg1.at[mine], local_sem)
    first.start()
    first.wait()
    gather(seg1, 0)
    seg2[mine] = multiply(seg1, 0).astype(jnp.bfloat16)
    gather(seg2, 1)
    filtered = 2.0 * multiply(seg2, 1) - start[...].astype(jnp.float32)
    filt[...] = filtered

    def to_group(source, target, group, count, me, device_of, whole):
        def send(i, carry):
            peer = lax.rem(me + i, count)
            pltpu.make_async_remote_copy(
                src_ref=source.at[peer if whole else me],
                dst_ref=target.at[me],
                send_sem=group_send.at[group],
                recv_sem=group_recv.at[group],
                device_id=device_of(peer),
                device_id_type=MESH,
            ).start()
            return carry

        lax.fori_loop(1, count, send, 0)
        wait_bytes(target.at[pl.ds(0, count - 1)], group_recv.at[group])
        wait_bytes(target.at[pl.ds(0, count - 1)], group_send.at[group])

    def sum_of(ref, count):
        total = ref[0]
        for i in range(1, count):
            total = total + ref[i]
        return total

    total = None
    for term in split3(filtered):
        product = lax.dot_general(
            hist[...], term, (((0,), (0,)), ((), ())), preferred_element_type=jnp.float32
        )
        total = product if total is None else total + product
    proj[...] = total.reshape(proj.shape)
    proj_in[place] = proj[place]
    to_group(proj, proj_in, 0, PLANE, place, plane_device, True)

    z_hi, z_lo = z // ZA, lax.rem(z, ZA)
    za_in[z_lo] = sum_of(proj_in, PLANE)
    to_group(za_in, za_in, 1, ZA, z_lo, lambda i: (xh, y, core, z_hi * ZA + i, xl), False)
    zb_in[z_hi] = sum_of(za_in, ZA)
    to_group(zb_in, zb_in, 2, ZB, z_hi, lambda i: (xh, y, core, i * ZA + z_lo, xl), False)
    coef[place] = sum_of(zb_in, ZB)
    to_group(coef, coef, 3, PLANE, place, plane_device, False)
    coeffs = coef[...].reshape(coef_out.shape)
    coef_out[...] = coeffs

    cleaned = filt[...]
    for term in split3(coeffs):
        cleaned = cleaned - jnp.dot(hist[...], term, preferred_element_type=jnp.float32)
    filt[...] = cleaned
    sq_plane[place] = jnp.sum(cleaned * cleaned, axis=0, keepdims=True)
    to_group(sq_plane, sq_plane, 4, PLANE, place, plane_device, False)
    sq_z[z] = sum_of(sq_plane, PLANE)
    to_group(sq_z, sq_z, 5, Z, z, lambda i: (xh, y, core, i, xl), False)
    lengths = jnp.sqrt(sum_of(sq_z, Z) / states + 1e-05)
    out[...] = filt[...] / lengths


def per_device(start_block, matrix_tiles, tile_columns, history):
    rows, width = start_block.shape
    vectors = history.shape[1]
    chunk = vectors // PLANE
    f32, bf16 = jnp.float32, jnp.bfloat16
    vmem = pl.BlockSpec(memory_space=pltpu.VMEM)
    return pl.pallas_call(
        functools.partial(kernel, float(rows * XH * Y * CORE * Z * XL)),
        out_shape=(
            jax.ShapeDtypeStruct((rows, width), f32),
            jax.ShapeDtypeStruct((vectors, width), f32),
        ),
        in_specs=[pl.BlockSpec(memory_space=pltpu.SMEM), vmem, vmem, vmem],
        out_specs=(vmem, vmem),
        scratch_shapes=[
            pltpu.VMEM((Z * XL, rows, width), bf16),
            pltpu.VMEM((Z * XL, rows, width), bf16),
            pltpu.VMEM((CORE, Y, XH, rows, width), f32),
            pltpu.VMEM((2, Y, XH, rows, width), f32),
            pltpu.VMEM((Y, XH, rows, width), f32),
            pltpu.VMEM((2, Y - 1, XH, rows, width), f32),
            pltpu.VMEM((XH, rows, width), f32),
            pltpu.VMEM((2, rows, width), f32),
            pltpu.VMEM((rows, width), f32),
            pltpu.VMEM((PLANE, chunk, width), f32),
            pltpu.VMEM((PLANE, chunk, width), f32),
            pltpu.VMEM((ZA, chunk, width), f32),
            pltpu.VMEM((ZB, chunk, width), f32),
            pltpu.VMEM((PLANE, chunk, width), f32),
            pltpu.VMEM((PLANE, 1, width), f32),
            pltpu.VMEM((Z, 1, width), f32),
            pltpu.SemaphoreType.DMA((2, 3)),
            pltpu.SemaphoreType.DMA((2, Z * XL)),
            pltpu.SemaphoreType.DMA((2, Y + 1)),
            pltpu.SemaphoreType.DMA((2, Y + 1)),
            pltpu.SemaphoreType.DMA((6,)),
            pltpu.SemaphoreType.DMA((6,)),
            pltpu.SemaphoreType.DMA,
        ],
        compiler_params=pltpu.CompilerParams(
            collective_id=0, has_side_effects=True, vmem_limit_bytes=40 * 1024 * 1024
        ),
    )(
        tile_columns.reshape(XH * Y * CORE, 2),
        start_block,
        matrix_tiles.reshape(XH * Y * CORE, 2, TILE, TILE),
        history,
    )


def solution(mesh):
    split = Mesh(mesh.devices.reshape(XH, Y, CORE, Z, XL), ROW_COL)
    return jax.shard_map(
        per_device,
        mesh=split,
        in_specs=(
            P(ROW_COL, None),
            P(ROW, None, COL, None, None, None),
            P(ROW, None, COL, None),
            P(ROW_COL, None),
        ),
        out_specs=(P(ROW_COL, None), P()),
        check_vma=False,
    )
```

time: 974 us -> 225 us (0.23); the launches traced: 961 us -> 225 us
  waiting for transfers between devices: 760 us -> 0 us
  Pallas kernels: 0 us -> 220 us
  blocking collectives: 172 us -> 0 us
  between operations: 14.2 us -> 0.65 us
    psum x5 -> x0, waiting for transfers between devices: 528 us -> none  [one_axis_at_a_time(): return functools.reduce(lax.psum, axes, value)]
    all_gather x2 -> x0, waiting for transfers between devices: 232 us -> none  [gathered_by_axis(): nearer = lax.all_gather(value, axes[-1], axis=dim, tiled=True)]
    pallas_call x0 -> x1, Pallas kernels: none -> 220 us  [per_device(): pl.pallas_call(functools.partial(kernel, float(rows * XH * Y * CORE * Z *...]
    all_to_all x2 -> x0, blocking collectives: 92.3 us -> none  [sum_at_owner(): lax.all_to_all(blocks, axis, split_axis=0, concat_axis=0, tiled=True)]
    psum x5 -> x0, blocking collectives: 70 us -> none  [one_axis_at_a_time(): return functools.reduce(lax.psum, axes, value)]
  transfers between devices with their start and end apart: 7 -> 0, of which waited for: 7 -> 0; matrix products, arithmetic and copies ran while one was open for 0% -> 0% of each run, Pallas kernels for 0% -> 0%
where the time goes in v1:
time: 225 us
  Pallas kernels  220 us (98%)
  local copies, waits for them, and re-layouts  4.97 us (2%)
    pallas_call x1, Pallas kernels, per_device(): pl.pallas_call(functools.partial(kernel, float(rows * XH * Y * CORE * Z *...  220 us
    unnamed x10, local copies, waits for them, and re-layouts  4.89 us

profile of v1, /device:TPU:1, one launch (start us, length us, event | category | flops | bytes accessed | tf_op | source)
XLA Modules:
  0.0 225.1 jit_solution(2535488983909294358)
XLA Ops:
  0.6 0.0 copy-start.3
  0.6 0.7 copy-done.3
  1.3 0.1 copy.6.cols
  1.4 0.0 copy-start
  1.4 1.2 copy-done
  2.6 0.0 copy-start.1
  2.6 0.9 copy-done.1
  3.5 0.0 copy-start.2
  3.5 0.8 copy-done.2
  4.3 219.5 %shard_map.59 = (f32[128,128]{1,0:T(8,128)S(1)}, f32[512,128]{1,0:T(8,128)S(1)}) custom-call(s32[16,2]{1,0:T(8,128)S(1)} %copy.6.cols, bf16[128,128]{1,0:T(8,128)(2,1)S(1)} %copy-done.2, bf16[16,2,128,128]{3,2,1,0:T(8,128)(2,1)S(1)} %bitcast.2, bf16[128,512]{1,0:T(8,128)(2,1)S(1)} %copy-done.1), custom_call_target="tpu_custom_call" | custom-call | tf_op jit(solution)/shard_map/pallas_call | solution.py:279
  223.8 0.6 copy.9
  224.4 0.7 copy.10
Async XLA Ops:
  0.6 0.7 copy-start.3
  1.4 1.2 copy-start
  2.6 0.9 copy-start.1
  3.5 0.8 copy-start.2

commit v2 on v1

--- a/solution.py
+++ b/solution.py
@@ -17,6 +17,7 @@
 ZB = Z // ZA
 PLANE = XH * XL * Y * CORE
 TILE = 128
+STRIDE = 4
 
 
 def split3(x):
@@ -34,11 +35,14 @@
 def kernel(
     states,
     cols,
+    start_hbm,
+    tiles_hbm,
+    hist_hbm,
+    out,
+    coef_out,
     start,
     tiles,
     hist,
-    out,
-    coef_out,
     seg1,
     seg2,
     part,
@@ -65,8 +69,10 @@
 ):
     xh, y, core = (lax.axis_index(a) for a in ROW)
     z, xl = (lax.axis_index(a) for a in COL)
-    right = (xh, y, core, lax.rem(z + 1, Z), xl)
-    left = (xh, y, core, lax.rem(z + Z - 1, Z), xl)
+
+    def along(step):
+        return (xh, y, core, lax.rem(z + step + Z, Z), xl)
+
     across = (xh, y, core, z, 1 - xl)
     place = ((xh * XL + xl) * Y + y) * CORE + core
 
@@ -79,6 +85,22 @@
             lax.rem(q // (Y * CORE), XL),
         )
 
+    def slot_of(zz):
+        return lax.rem(zz + 2 * Z, Z) * XL + xl
+
+    mine = slot_of(z)
+    first = pltpu.make_async_copy(start_hbm, seg1.at[mine], local_sem.at[0])
+    first.start()
+    loads = [
+        pltpu.make_async_copy(source, target, local_sem.at[i])
+        for i, source, target in (
+            (1, tiles_hbm, tiles),
+            (2, hist_hbm, hist),
+            (3, start_hbm, start),
+        )
+    ]
+    for load in loads:
+        load.start()
     barrier = pltpu.get_barrier_semaphore()
 
     def greet(i, carry):
@@ -86,16 +108,17 @@
         pl.semaphore_signal(barrier, inc=1, device_id=device, device_id_type=MESH)
         return carry
 
-    for device in (left, right):
-        pl.semaphore_signal(barrier, inc=1, device_id=device, device_id_type=MESH)
+    for reach in (STRIDE, 2, 1):
+        for device in (along(reach), along(-reach)):
+            pl.semaphore_signal(
+                barrier, inc=1, device_id=device, device_id_type=MESH
+            )
     lax.fori_loop(1, PLANE, greet, 0)
-    pl.semaphore_wait(barrier, PLANE + 1)
-
-    def slot_of(zz):
-        return lax.rem(zz + Z, Z) * XL + xl
+    pl.semaphore_wait(barrier, PLANE + 5)
 
     def gather(seg, which):
-        def send(slot, device, lane):
+        def send(offset, device, lane):
+            slot = slot_of(z + offset)
             pltpu.make_async_remote_copy(
                 src_ref=seg.at[slot],
                 dst_ref=seg.at[slot],
@@ -105,48 +128,84 @@
                 device_id_type=MESH,
             ).start()
 
-        def arrived(slot):
+        def arrived(offset):
+            slot = slot_of(z + offset)
             wait_bytes(seg.at[slot], ring_recv.at[which, slot])
 
-        def step(k, carry):
-            ahead, behind = slot_of(z - k), slot_of(z + k)
-            send(ahead, right, 0)
-            send(behind, left, 1)
-            send(ahead, across, 2)
+        def cross(*offsets):
+            for offset in offsets:
+                arrived(offset)
+                send(offset, across, 4)
+
+        def spread(k):
+            for near in (1, -1):
+                send(-STRIDE * k, along(near), 2)
+                send(STRIDE * k, along(near), 3)
+            send(-STRIDE * k, along(2), 2)
+            send(STRIDE * k, along(-2), 3)
+
+        def spread_in(k):
+            cross(-1 - STRIDE * k, 1 + STRIDE * k, -2 - STRIDE * k, 2 + STRIDE * k)
 
             @pl.when(k > 0)
             def _():
-                send(behind, across, 2)
-
-            arrived(slot_of(z - k - 1))
-            arrived(slot_of(z + k + 1))
+                cross(-1 + STRIDE * k, 1 - STRIDE * k)
+
+        def step(k, carry):
+            arrived(-STRIDE * k)
+            send(-STRIDE * k, along(STRIDE), 0)
+            arrived(STRIDE * k)
+            send(STRIDE * k, along(-STRIDE), 1)
+            spread(k)
+            send(-STRIDE * k, across, 4)
+            send(STRIDE * k, across, 4)
+            spread_in(k - 1)
             return carry
 
-        half = Z // 2
-        lax.fori_loop(0, half - 1, step, 0)
-        send(slot_of(z - half + 1), right, 0)
-        send(slot_of(z - half + 1), across, 2)
-        send(slot_of(z + half - 1), across, 2)
-        arrived(slot_of(z - half))
-        send(slot_of(z - half), across, 2)
+        last = Z // 2 // STRIDE - 1
+        far = Z // 2
+        send(0, along(STRIDE), 0)
+        send(0, along(-STRIDE), 1)
+        send(0, along(1), 2)
+        send(0, along(-1), 3)
+        send(0, along(2), 2)
+        send(0, along(-2), 3)
+        send(0, across, 4)
+        lax.fori_loop(1, last, step, 0)
+        arrived(-STRIDE * last)
+        send(-STRIDE * last, along(STRIDE), 0)
+        arrived(STRIDE * last)
+        spread(last)
+        send(-STRIDE * last, across, 4)
+        send(STRIDE * last, across, 4)
+        spread_in(jnp.int32(last - 1))
+        arrived(-far)
+        send(-far, along(1), 2)
+        send(-far, along(-1), 3)
+        send(-far, across, 4)
+        spread_in(jnp.int32(last))
+        cross(far - 1, 1 - far)
 
         def other(zz, carry):
-            arrived(zz * XL + 1 - xl)
+            slot = zz * XL + 1 - xl
+            wait_bytes(seg.at[slot], ring_recv.at[which, slot])
             return carry
 
         lax.fori_loop(0, Z, other, 0)
-        wait_bytes(seg.at[pl.ds(0, half)], ring_send.at[which, 0])
-        wait_bytes(seg.at[pl.ds(0, half - 1)], ring_send.at[which, 1])
-        wait_bytes(seg.at[pl.ds(0, Z)], ring_send.at[which, 2])
+        wait_bytes(seg.at[pl.ds(0, last + 1)], ring_send.at[which, 0])
+        wait_bytes(seg.at[pl.ds(0, last)], ring_send.at[which, 1])
+        wait_bytes(seg.at[pl.ds(0, 3 * last + 3)], ring_send.at[which, 2])
+        wait_bytes(seg.at[pl.ds(0, 3 * last + 3)], ring_send.at[which, 3])
+        wait_bytes(seg.at[pl.ds(0, Z)], ring_send.at[which, 4])
 
     def multiply(seg, which):
         def one(owner_core, yy, xx):
             p = (xx * Y + yy) * CORE + owner_core
             total = jnp.dot(
-                tiles[p, 0], seg[cols[p, 0]], preferred_element_type=jnp.float32
+                tiles[p, 0], seg[cols[0, p]], preferred_element_type=jnp.float32
             )
             total += jnp.dot(
-                tiles[p, 1], seg[cols[p, 1]], preferred_element_type=jnp.float32
+                tiles[p, 1], seg[cols[1, p]], preferred_element_type=jnp.float32
             )
             part[owner_core, yy, xx] = total
 
@@ -205,11 +264,10 @@
         last.wait()
         return pair[xh] + x_in[which]
 
-    mine = slot_of(z)
-    first = pltpu.make_async_copy(start, seg1.at[mine], local_sem)
-    first.start()
     first.wait()
     gather(seg1, 0)
+    for load in loads:
+        load.wait()
     seg2[mine] = multiply(seg1, 0).astype(jnp.bfloat16)
     gather(seg2, 1)
     filtered = 2.0 * multiply(seg2, 1) - start[...].astype(jnp.float32)
@@ -276,15 +334,19 @@
     chunk = vectors // PLANE
     f32, bf16 = jnp.float32, jnp.bfloat16
     vmem = pl.BlockSpec(memory_space=pltpu.VMEM)
+    any_space = pl.BlockSpec(memory_space=pl.ANY)
     return pl.pallas_call(
         functools.partial(kernel, float(rows * XH * Y * CORE * Z * XL)),
         out_shape=(
             jax.ShapeDtypeStruct((rows, width), f32),
             jax.ShapeDtypeStruct((vectors, width), f32),
         ),
-        in_specs=[pl.BlockSpec(memory_space=pltpu.SMEM), vmem, vmem, vmem],
+        in_specs=[pl.BlockSpec(memory_space=pltpu.SMEM), any_space, any_space, any_space],
         out_specs=(vmem, vmem),
         scratch_shapes=[
+            pltpu.VMEM((rows, width), bf16),
+            pltpu.VMEM((XH * Y * CORE, 2, TILE, TILE), bf16),
+            pltpu.VMEM((rows, vectors), bf16),
             pltpu.VMEM((Z * XL, rows, width), bf16),
             pltpu.VMEM((Z * XL, rows, width), bf16),
             pltpu.VMEM((CORE, Y, XH, rows, width), f32),
@@ -301,19 +363,19 @@
             pltpu.VMEM((PLANE, chunk, width), f32),
             pltpu.VMEM((PLANE, 1, width), f32),
             pltpu.VMEM((Z, 1, width), f32),
-            pltpu.SemaphoreType.DMA((2, 3)),
+            pltpu.SemaphoreType.DMA((2, 5)),
             pltpu.SemaphoreType.DMA((2, Z * XL)),
             pltpu.SemaphoreType.DMA((2, Y + 1)),
             pltpu.SemaphoreType.DMA((2, Y + 1)),
             pltpu.SemaphoreType.DMA((6,)),
             pltpu.SemaphoreType.DMA((6,)),
-            pltpu.SemaphoreType.DMA,
+            pltpu.SemaphoreType.DMA((4,)),
         ],
         compiler_params=pltpu.CompilerParams(
-            collective_id=0, has_side_effects=True, vmem_limit_bytes=40 * 1024 * 1024
+            collective_id=0, has_side_effects=True, vmem_limit_bytes=56 * 1024 * 1024
         ),
     )(
-        tile_columns.reshape(XH * Y * CORE, 2),
+        tile_columns.reshape(XH * Y * CORE, 2).T,
         start_block,
         matrix_tiles.reshape(XH * Y * CORE, 2, TILE, TILE),
         history,

time: 225 us -> 169 us (0.75)
  Pallas kernels: 220 us -> 165 us
    pallas_call x1, Pallas kernels: 220 us -> 165 us  [per_device(): pl.pallas_call(functools.partial(kernel, float(rows * XH * Y * CORE * Z *...]
    unnamed x10 -> x2, local copies, waits for them, and re-layouts: 4.89 us -> 3.14 us
where the time goes in v2:
time: 169 us; the launch traced here: 168 us
  Pallas kernels  165 us (98%)
  local copies, waits for them, and re-layouts  3.14 us (2%)
    pallas_call x1, Pallas kernels, per_device(): pl.pallas_call(functools.partial(kernel, float(rows * XH * Y * CORE * Z *...  165 us

profile of v2, /device:TPU:1, one launch (start us, length us, event | category | flops | bytes accessed | tf_op | source)
XLA Modules:
  0.0 168.5 jit_solution(8540233098999005223)
XLA Ops:
  0.6 164.7 %shard_map.59 = (f32[128,128]{1,0:T(8,128)}, f32[512,128]{1,0:T(8,128)}) custom-call(s32[2,16]{1,0:T(2,128)} %bitcast.5, bf16[128,128]{1,0:T(8,128)(2,1)} %start_hbm.1, bf16[16,2,128,128]{3,2,1,0:T(8,128)(2,1)} %bitcast.4, bf16[128,512]{1,0:T(8,128)(2,1)} %hist_hbm.1), custom_call_target="tpu_custom_call" | custom-call | tf_op jit(solution)/shard_map/pallas_call | solution.py:338
  165.4 1.5 copy.8
  166.8 1.7 copy.9

commit v3 on v2

--- a/solution.py
+++ b/solution.py
@@ -47,10 +47,14 @@
     seg2,
     part,
     core_in,
-    summed,
-    y_in,
+    upper,
+    lower,
+    ya_in,
+    yb_in,
+    xa_in,
+    xb_in,
     pair,
-    x_in,
+    crossed,
     filt,
     proj,
     proj_in,
@@ -199,70 +203,82 @@
         wait_bytes(seg.at[pl.ds(0, Z)], ring_send.at[which, 4])
 
     def multiply(seg, which):
-        def one(owner_core, yy, xx):
-            p = (xx * Y + yy) * CORE + owner_core
-            total = jnp.dot(
-                tiles[p, 0], seg[cols[0, p]], preferred_element_type=jnp.float32
+        def blocks(owner_core, yy):
+            for xx in range(XH):
+                p = (xx * Y + yy) * CORE + owner_core
+                left = jnp.concatenate([tiles[p, 0], tiles[p, 1]], axis=1)
+                right = jnp.concatenate([seg[cols[0, p]], seg[cols[1, p]]], axis=0)
+                yield xx, jnp.dot(left, right, preferred_element_type=jnp.float32)
+
+        def push(source, target, lane, device):
+            copy = pltpu.make_async_remote_copy(
+                src_ref=source,
+                dst_ref=target,
+                send_sem=row_send.at[which, lane],
+                recv_sem=row_recv.at[which, lane],
+                device_id=device,
+                device_id_type=MESH,
             )
-            total += jnp.dot(
-                tiles[p, 1], seg[cols[1, p]], preferred_element_type=jnp.float32
+            copy.start()
+            return copy
+
+        def row_of(i):
+            return lax.rem(y + i, Y)
+
+        def y_device(i):
+            return (xh, row_of(i), core, z, xl)
+
+        other_core = (xh, y, 1 - core, z, xl)
+        other_x = (1 - xh, y, core, z, xl)
+        order = (2, 1, 3, 0)
+        half = TILE // 2
+        swaps, y_first, x_first = {}, {}, {}
+        for i in order:
+            yy = row_of(i)
+            for xx, value in blocks(1 - core, yy):
+                part[yy, xx] = value
+            swaps[i] = push(part.at[yy], core_in.at[which, yy], i, other_core)
+        for i in order:
+            yy = row_of(i)
+            mine_here = list(blocks(core, yy))
+            swaps[i].wait_recv()
+            for xx, value in mine_here:
+                value = value + core_in[which, yy, xx]
+                upper[yy, xx] = value[:half]
+                lower[yy, xx] = value[half:]
+            x_first[i] = push(
+                lower.at[yy, 1 - xh], xb_in.at[which, yy], 2 * Y + i, other_x
             )
-            part[owner_core, yy, xx] = total
-
-        def half_of(owner_core):
-            def body(yy, carry):
-                for xx in range(XH):
-                    one(owner_core, yy, xx)
-                return carry
-
-            lax.fori_loop(0, Y, body, 0)
-
-        half_of(1 - core)
-        swap = pltpu.make_async_remote_copy(
-            src_ref=part.at[1 - core],
-            dst_ref=core_in.at[which],
-            send_sem=row_send.at[which, 0],
-            recv_sem=row_recv.at[which, 0],
-            device_id=(xh, y, 1 - core, z, xl),
-            device_id_type=MESH,
-        )
-        swap.start()
-        half_of(core)
-        swap.wait()
-
-        def add_up(yy, carry):
-            summed[yy] = part[core, yy] + core_in[which, yy]
-            return carry
-
-        lax.fori_loop(0, Y, add_up, 0)
-        hops = []
-        for i in (2, 1, 3):
-            hops.append(
-                pltpu.make_async_remote_copy(
-                    src_ref=summed.at[lax.rem(y + i, Y)],
-                    dst_ref=y_in.at[which, i - 1],
-                    send_sem=row_send.at[which, i],
-                    recv_sem=row_recv.at[which, i],
-                    device_id=(xh, lax.rem(y + i, Y), core, z, xl),
-                    device_id_type=MESH,
+            if i:
+                y_first[i] = push(
+                    upper.at[yy], ya_in.at[which, i - 1], Y + i, y_device(i)
                 )
+        for i in order[:3]:
+            y_first[i].wait_recv()
+        for xx in range(XH):
+            pair[xx] = (
+                upper[y, xx]
+                + ya_in[which, 0, xx]
+                + ya_in[which, 1, xx]
+                + ya_in[which, 2, xx]
             )
-        for hop in hops:
-            hop.start()
-        for hop in hops:
-            hop.wait()
-        pair[...] = summed[y] + y_in[which, 0] + y_in[which, 1] + y_in[which, 2]
-        last = pltpu.make_async_remote_copy(
-            src_ref=pair.at[1 - xh],
-            dst_ref=x_in.at[which],
-            send_sem=row_send.at[which, Y],
-            recv_sem=row_recv.at[which, Y],
-            device_id=(1 - xh, y, core, z, xl),
-            device_id_type=MESH,
-        )
-        last.start()
-        last.wait()
-        return pair[xh] + x_in[which]
+        x_last = push(pair.at[1 - xh], xa_in.at[which], Y, other_x)
+        for i in order:
+            x_first[i].wait_recv()
+        for yy in range(Y):
+            crossed[yy] = lower[yy, xh] + xb_in[which, yy]
+        y_last = [
+            push(crossed.at[row_of(i)], yb_in.at[which, i - 1], 3 * Y + i, y_device(i))
+            for i in order[:3]
+        ]
+        x_last.wait_recv()
+        top = pair[xh] + xa_in[which]
+        for copy in y_last:
+            copy.wait_recv()
+        bottom = crossed[y] + yb_in[which, 0] + yb_in[which, 1] + yb_in[which, 2]
+        for copy in (*swaps.values(), *x_first.values(), *y_first.values(), x_last, *y_last):
+            copy.wait_send()
+        return jnp.concatenate([top, bottom], axis=0)
 
     first.wait()
     gather(seg1, 0)
@@ -334,14 +350,14 @@
     chunk = vectors // PLANE
     f32, bf16 = jnp.float32, jnp.bfloat16
     vmem = pl.BlockSpec(memory_space=pltpu.VMEM)
-    any_space = pl.BlockSpec(memory_space=pl.ANY)
+    hbm = pl.BlockSpec(memory_space=pl.ANY)
     return pl.pallas_call(
         functools.partial(kernel, float(rows * XH * Y * CORE * Z * XL)),
         out_shape=(
             jax.ShapeDtypeStruct((rows, width), f32),
             jax.ShapeDtypeStruct((vectors, width), f32),
         ),
-        in_specs=[pl.BlockSpec(memory_space=pltpu.SMEM), any_space, any_space, any_space],
+        in_specs=[pl.BlockSpec(memory_space=pltpu.SMEM), hbm, hbm, hbm],
         out_specs=(vmem, vmem),
         scratch_shapes=[
             pltpu.VMEM((rows, width), bf16),
@@ -349,12 +365,16 @@
             pltpu.VMEM((rows, vectors), bf16),
             pltpu.VMEM((Z * XL, rows, width), bf16),
             pltpu.VMEM((Z * XL, rows, width), bf16),
-            pltpu.VMEM((CORE, Y, XH, rows, width), f32),
+            pltpu.VMEM((Y, XH, rows, width), f32),
             pltpu.VMEM((2, Y, XH, rows, width), f32),
-            pltpu.VMEM((Y, XH, rows, width), f32),
-            pltpu.VMEM((2, Y - 1, XH, rows, width), f32),
-            pltpu.VMEM((XH, rows, width), f32),
-            pltpu.VMEM((2, rows, width), f32),
+            pltpu.VMEM((Y, XH, rows // 2, width), f32),
+            pltpu.VMEM((Y, XH, rows // 2, width), f32),
+            pltpu.VMEM((2, Y - 1, XH, rows // 2, width), f32),
+            pltpu.VMEM((2, Y - 1, rows // 2, width), f32),
+            pltpu.VMEM((2, rows // 2, width), f32),
+            pltpu.VMEM((2, Y, rows // 2, width), f32),
+            pltpu.VMEM((XH, rows // 2, width), f32),
+            pltpu.VMEM((Y, rows // 2, width), f32),
             pltpu.VMEM((rows, width), f32),
             pltpu.VMEM((PLANE, chunk, width), f32),
             pltpu.VMEM((PLANE, chunk, width), f32),
@@ -365,14 +385,14 @@
             pltpu.VMEM((Z, 1, width), f32),
             pltpu.SemaphoreType.DMA((2, 5)),
             pltpu.SemaphoreType.DMA((2, Z * XL)),
-            pltpu.SemaphoreType.DMA((2, Y + 1)),
-            pltpu.SemaphoreType.DMA((2, Y + 1)),
+            pltpu.SemaphoreType.DMA((2, 4 * Y)),
+            pltpu.SemaphoreType.DMA((2, 4 * Y)),
             pltpu.SemaphoreType.DMA((6,)),
             pltpu.SemaphoreType.DMA((6,)),
             pltpu.SemaphoreType.DMA((4,)),
         ],
         compiler_params=pltpu.CompilerParams(
-            collective_id=0, has_side_effects=True, vmem_limit_bytes=56 * 1024 * 1024
+            collective_id=0, has_side_effects=True, vmem_limit_bytes=58720256
         ),
     )(
         tile_columns.reshape(XH * Y * CORE, 2).T,

time: 169 us -> 162 us (0.959)
  Pallas kernels: 165 us -> 158 us
    pallas_call x1, Pallas kernels: 165 us -> 158 us  [per_device(): pl.pallas_call(functools.partial(kernel, float(rows * XH * Y * CORE * Z *...]
where the time goes in v3:
time: 162 us
  Pallas kernels  158 us (98%)
  local copies, waits for them, and re-layouts  3.14 us (2%)
    pallas_call x1, Pallas kernels, per_device(): pl.pallas_call(functools.partial(kernel, float(rows * XH * Y * CORE * Z *...  158 us

profile of v3, /device:TPU:1, one launch (start us, length us, event | category | flops | bytes accessed | tf_op | source)
XLA Modules:
  0.0 161.9 jit_solution(5865150183923202506)
XLA Ops:
  0.6 158.1 %shard_map.59 = (f32[128,128]{1,0:T(8,128)}, f32[512,128]{1,0:T(8,128)}) custom-call(s32[2,16]{1,0:T(2,128)} %bitcast.5, bf16[128,128]{1,0:T(8,128)(2,1)} %start_hbm.1, bf16[16,2,128,128]{3,2,1,0:T(8,128)(2,1)} %bitcast.4, bf16[128,512]{1,0:T(8,128)(2,1)} %hist_hbm.1), custom_call_target="tpu_custom_call" | custom-call | tf_op jit(solution)/shard_map/pallas_call | solution.py:354
  158.7 1.5 copy.8
  160.2 1.7 %copy.9 = f32[512,128]{1,0:T(8,128)} copy(f32[512,128]{1,0:T(8,128)} %get-tuple-element.5) | data formatting | bytes 524288

commit v4 on v3

--- a/solution.py
+++ b/solution.py
@@ -82,11 +82,11 @@
 
     def plane_device(q):
         return (
-            q // (XL * Y * CORE),
-            lax.rem(q // CORE, Y),
+            lax.div(q, XL * Y * CORE),
+            lax.rem(lax.div(q, CORE), Y),
             lax.rem(q, CORE),
             z,
-            lax.rem(q // (Y * CORE), XL),
+            lax.rem(lax.div(q, Y * CORE), XL),
         )
 
     def slot_of(zz):
@@ -119,6 +119,8 @@
             )
     lax.fori_loop(1, PLANE, greet, 0)
     pl.semaphore_wait(barrier, PLANE + 5)
+
+    unsent = []
 
     def gather(seg, which):
         def send(offset, device, lane):
@@ -196,11 +198,9 @@
             return carry
 
         lax.fori_loop(0, Z, other, 0)
-        wait_bytes(seg.at[pl.ds(0, last + 1)], ring_send.at[which, 0])
-        wait_bytes(seg.at[pl.ds(0, last)], ring_send.at[which, 1])
-        wait_bytes(seg.at[pl.ds(0, 3 * last + 3)], ring_send.at[which, 2])
-        wait_bytes(seg.at[pl.ds(0, 3 * last + 3)], ring_send.at[which, 3])
-        wait_bytes(seg.at[pl.ds(0, Z)], ring_send.at[which, 4])
+        counts = (last + 1, last, 3 * last + 3, 3 * last + 3, Z)
+        for lane, count in enumerate(counts):
+            unsent.append((seg.at[pl.ds(0, count)], ring_send.at[which, lane]))
 
     def multiply(seg, which):
         def blocks(owner_core, yy):
@@ -276,22 +276,28 @@
         for copy in y_last:
             copy.wait_recv()
         bottom = crossed[y] + yb_in[which, 0] + yb_in[which, 1] + yb_in[which, 2]
-        for copy in (*swaps.values(), *x_first.values(), *y_first.values(), x_last, *y_last):
-            copy.wait_send()
-        return jnp.concatenate([top, bottom], axis=0)
+        sent = (*swaps.values(), *x_first.values(), *y_first.values(), x_last, *y_last)
+        return jnp.concatenate([top, bottom], axis=0), sent
 
     first.wait()
     gather(seg1, 0)
     for load in loads:
         load.wait()
-    seg2[mine] = multiply(seg1, 0).astype(jnp.bfloat16)
+    first_power, sent = multiply(seg1, 0)
+    seg2[mine] = first_power.astype(jnp.bfloat16)
     gather(seg2, 1)
-    filtered = 2.0 * multiply(seg2, 1) - start[...].astype(jnp.float32)
+    for copy in sent:
+        copy.wait_send()
+    second_power, sent = multiply(seg2, 1)
+    filtered = 2.0 * second_power - start[...].astype(jnp.float32)
     filt[...] = filtered
+
+    def far_first(i, count):
+        return jnp.where(i <= count // 2, count // 2 + 1 - i, i)
 
     def to_group(source, target, group, count, me, device_of, whole):
         def send(i, carry):
-            peer = lax.rem(me + i, count)
+            peer = lax.rem(me + far_first(i, count), count)
             pltpu.make_async_remote_copy(
                 src_ref=source.at[peer if whole else me],
                 dst_ref=target.at[me],
@@ -304,7 +310,7 @@
 
         lax.fori_loop(1, count, send, 0)
         wait_bytes(target.at[pl.ds(0, count - 1)], group_recv.at[group])
-        wait_bytes(target.at[pl.ds(0, count - 1)], group_send.at[group])
+        unsent.append((target.at[pl.ds(0, count - 1)], group_send.at[group]))
 
     def sum_of(ref, count):
         total = ref[0]
@@ -330,7 +336,6 @@
     coef[place] = sum_of(zb_in, ZB)
     to_group(coef, coef, 3, PLANE, place, plane_device, False)
     coeffs = coef[...].reshape(coef_out.shape)
-    coef_out[...] = coeffs
 
     cleaned = filt[...]
     for term in split3(coeffs):
@@ -338,10 +343,15 @@
     filt[...] = cleaned
     sq_plane[place] = jnp.sum(cleaned * cleaned, axis=0, keepdims=True)
     to_group(sq_plane, sq_plane, 4, PLANE, place, plane_device, False)
+    coef_out[...] = coef[...].reshape(coef_out.shape)
     sq_z[z] = sum_of(sq_plane, PLANE)
     to_group(sq_z, sq_z, 5, Z, z, lambda i: (xh, y, core, i, xl), False)
     lengths = jnp.sqrt(sum_of(sq_z, Z) / states + 1e-05)
     out[...] = filt[...] / lengths
+    for copy in sent:
+        copy.wait_send()
+    for ref, sem in unsent:
+        wait_bytes(ref, sem)
 
 
 def per_device(start_block, matrix_tiles, tile_columns, history):

time: 162 us -> 162 us (level)
  no operation moved by 1% of the time
where the time goes in v4:
time: 162 us
  Pallas kernels  158 us (98%)
  local copies, waits for them, and re-layouts  3.14 us (2%)
    pallas_call x1, Pallas kernels, per_device(): pl.pallas_call(functools.partial(kernel, float(rows * XH * Y * CORE * Z *...  158 us

profile of v4, /device:TPU:1, one launch (start us, length us, event | category | flops | bytes accessed | tf_op | source)
XLA Modules:
  0.0 161.9 jit_solution(12101135201388982248)
XLA Ops:
  0.6 158.1 %shard_map.59 = (f32[128,128]{1,0:T(8,128)}, f32[512,128]{1,0:T(8,128)}) custom-call(s32[2,16]{1,0:T(2,128)} %bitcast.5, bf16[128,128]{1,0:T(8,128)(2,1)} %start_hbm.1, bf16[16,2,128,128]{3,2,1,0:T(8,128)(2,1)} %bitcast.4, bf16[128,512]{1,0:T(8,128)(2,1)} %hist_hbm.1), custom_call_target="tpu_custom_call" | custom-call | tf_op jit(solution)/shard_map/pallas_call | solution.py:364
  158.7 1.5 copy.8
  160.2 1.7 %copy.9 = f32[512,128]{1,0:T(8,128)} copy(f32[512,128]{1,0:T(8,128)} %get-tuple-element.5) | data formatting | bytes 524288
